TPU v7x, 32 devices: a whole 2x2x4 slice. The times are simulated.
32 devices in a mesh: dp: 4 (over x, core), seq: 8 (over z, y).
Axes of the slice: x: 2, y: 2, z: 4, core: 2. Of those that a mesh axis runs over, the one named last changes fastest.
Arguments:
- tokens: bfloat16 [32768, 1152], P(('dp', 'seq')), may hold values from -6 to 6
- condition: bfloat16 [128, 1152], P('dp'), may hold values from -6 to 6
- lengths: int32 [128], P(('dp', 'seq')), may hold values from 1 to 256, 22937 in all
- kept_index: int32 [128, 256], P(('dp', 'seq')), may hold values from 0 to 255, each once within a row
- heads_weight: bfloat16 [1152, 3456], P('seq'), may hold values from -0.1875 to 0.1875
- heads_bias: bfloat16 [2304], replicated, may hold values from -1.5 to 1.5
- merge_weight: bfloat16 [1152, 1152], P('seq'), may hold values from -1.5 to 1.5
- merge_bias: bfloat16 [1152], replicated, may hold values from -4 to 4
- up_weight: bfloat16 [1152, 4608], P('seq'), may hold values from -0.1875 to 0.1875
- up_bias: bfloat16 [4608], replicated, may hold values from -4 to 4
- down_weight: bfloat16 [1152, 4608], P('seq'), may hold values from -0.1875 to 0.1875
- down_bias: bfloat16 [1152], replicated, may hold values from -4 to 4
- modulate_weight: bfloat16 [1152, 6912], P('seq'), may hold values from -0.1875 to 0.1875
- modulate_bias: bfloat16 [6912], replicated, may hold values from -4 to 4
- relative_table: bfloat16 [16, 961], replicated, may hold values from -6 to 6
- cotangent: bfloat16 [32768, 1152], P(('dp', 'seq')), may hold values from -6 to 6
Outputs:
- output: bfloat16 [32768, 1152], P(('dp', 'seq'))
- tokens_grad: float32 [32768, 1152], P(('dp', 'seq'))
- heads_weight_grad: float32 [1152, 3456], P('seq')
- merge_weight_grad: float32 [1152, 1152], P('seq')
- up_weight_grad: float32 [1152, 4608], P('seq')
- down_weight_grad: float32 [1152, 4608], P('seq')
- modulate_weight_grad: float32 [1152, 6912], P('seq')
- heads_bias_grad: float32 [2304], replicated
- merge_bias_grad: float32 [1152], replicated
- up_bias_grad: float32 [4608], replicated
- down_bias_grad: float32 [1152], replicated
- modulate_bias_grad: float32 [6912], replicated
- relative_table_grad: float32 [16, 961], replicated
Inputs may be any that keep to these rules, and one draw needn't show every extreme that they name: The first lengths[s] slots of sample s hold its kept tokens, the rest are empty. Each sample's row is a permutation of the 256 patch positions; slot r's patch lies at row kept_index // 16, column kept_index % 16.
All inputs are finite; a program needn't handle non-finite values. No bound on the sum of `lengths` on one device may be relied on, other than what follows from the above.
Results may differ from a plain program's by a relative error of at most 0.019.
Values may be sent and summed in bfloat16 or wider, within the bound.
No kernel may reach another device: no remote copies, remote signals or barrier semaphores. Data moves between devices by JAX's collectives and lax.ppermute only.
A program may use at most 320 MiB of HBM per device.

v0:
```python
from functools import partial
import math
import jax
import jax.numpy as jnp
from jax import lax
from jax.sharding import PartitionSpec as P

D = 1152
HEADS = 16
HEAD = 72
FF = 4608
SIDE = 16
MICRO = 2
SAMP_DEV = 4
GRID = 256
epsilon = 1e-06


def layer_norm(values):
    center = values - jnp.mean(values, axis=-1, keepdims=True)
    spread = jnp.mean(center * center, axis=-1, keepdims=True)
    return center * lax.rsqrt(spread + epsilon)


def modulated(values, scales, shifts):
    return layer_norm(values) * (1.0 + scales) + shifts


def gelu_tanh(values):
    return jax.nn.gelu(values, approximate=True)


def fold_rows(left, portion):
    return jnp.dot(left, portion, preferred_element_type=jnp.float32)


def right_transposed(left, portion):
    return lax.dot_general(
        left, portion, (((1,), (1,)), ((), ())), preferred_element_type=jnp.float32
    )


def column_outer(left, right):
    return lax.dot_general(
        left, right, (((0,), (0,)), ((), ())), preferred_element_type=jnp.float32
    )


def relative_index(positions):
    row_place = positions // SIDE
    col_place = positions % SIDE
    row_gap = row_place[..., :, None] - row_place[..., None, :] + (SIDE - 1)
    col_gap = col_place[..., :, None] - col_place[..., None, :] + (SIDE - 1)
    return row_gap * (2 * SIDE - 1) + col_gap


def slot_onehot(index_pair):
    return (index_pair[..., :, None] == jnp.arange(GRID)[None, None, :]).astype(jnp.bfloat16)


def pair_scores(packed, lens_pair, index_pair, position_bias):
    parts = packed.reshape(2, GRID, 3, HEADS, HEAD)
    queries = parts[:, :, 0]
    key_part = parts[:, :, 1]
    value_part = parts[:, :, 2]
    scaling = 1.0 / math.sqrt(HEAD)
    onehot = slot_onehot(index_pair)
    rows_placed = jnp.einsum(
        "srp,hpq->hsrq", onehot, position_bias, preferred_element_type=jnp.float32
    ).astype(jnp.bfloat16)
    bias_pair = jnp.einsum(
        "hsrq,skq->hsrk", rows_placed, onehot, preferred_element_type=jnp.float32
    )
    scores = (
        jnp.einsum("sqhe,skhe->hsqk", queries, key_part, preferred_element_type=jnp.float32)
        * scaling
    )
    scores = scores + bias_pair
    living = jnp.arange(GRID)[None, :] < lens_pair[:, None]
    scores = jnp.where(living[None, :, None, :], scores, -1e30)
    return (scores, queries, key_part, value_part, onehot)


def attend_pair(arguments, position_bias):
    packed, lens_pair, index_pair = arguments
    scores, queries, key_part, value_part, onehot = pair_scores(
        packed, lens_pair, index_pair, position_bias
    )
    peak = jnp.max(scores, axis=-1, keepdims=True)
    expo = jnp.exp(scores - peak)
    mass = jnp.sum(expo, axis=-1, keepdims=True)
    probs_low = (expo / mass).astype(jnp.bfloat16)
    mixed = jnp.einsum("hsqk,skhe->sqhe", probs_low, value_part, preferred_element_type=jnp.float32)
    return (mixed.astype(jnp.bfloat16).reshape(2 * GRID, D), (peak + jnp.log(mass))[..., 0])


def attend_pair_back(arguments, position_bias):
    packed, lens_pair, index_pair, logsum, grad_mixed = arguments
    scores, queries, key_part, value_part, onehot = pair_scores(
        packed, lens_pair, index_pair, position_bias
    )
    probs = jnp.exp(scores - logsum[..., None])
    grad_mixed = grad_mixed.reshape(2, GRID, HEADS, HEAD)
    grad_probs = jnp.einsum(
        "sqhe,skhe->hsqk", grad_mixed, value_part, preferred_element_type=jnp.float32
    )
    inner = jnp.sum(probs * grad_probs, axis=-1, keepdims=True)
    grad_scores = (probs * (grad_probs - inner)).astype(jnp.bfloat16)
    scaling = 1.0 / math.sqrt(HEAD)
    grad_query = (
        jnp.einsum("hsqk,skhe->sqhe", grad_scores, key_part, preferred_element_type=jnp.float32)
        * scaling
    )
    grad_key = (
        jnp.einsum("hsqk,sqhe->skhe", grad_scores, queries, preferred_element_type=jnp.float32)
        * scaling
    )
    grad_value = jnp.einsum(
        "hsqk,sqhe->skhe",
        probs.astype(jnp.bfloat16),
        grad_mixed,
        preferred_element_type=jnp.float32,
    )
    stacked = (
        jnp.stack([grad_query, grad_key, grad_value], axis=2)
        .astype(jnp.bfloat16)
        .reshape(2 * GRID, 3 * D)
    )
    rows_back = jnp.einsum(
        "hsrk,srp->hspk", grad_scores, onehot, preferred_element_type=jnp.float32
    ).astype(jnp.bfloat16)
    placed_grad = jnp.einsum("hspk,skq->hpq", rows_back, onehot, preferred_element_type=jnp.float32)
    return (stacked, placed_grad)


def offsets_table(placed_grad):
    spots = jnp.arange(SIDE)
    reach = jnp.arange(2 * SIDE - 1)
    gaps = (
        spots[:, None, None] - spots[None, :, None] + (SIDE - 1) == reach[None, None, :]
    ).astype(jnp.float32)
    grid_grad = placed_grad.reshape(HEADS, SIDE, SIDE, SIDE, SIDE)
    by_rows = jnp.einsum("hwxyz,wya->haxz", grid_grad, gaps, precision=lax.Precision.HIGHEST)
    return jnp.einsum("haxz,xzb->hab", by_rows, gaps, precision=lax.Precision.HIGHEST).reshape(
        HEADS, (2 * SIDE - 1) ** 2
    )


def local(
    tokens,
    condition,
    lengths,
    kept_index,
    heads_weight,
    heads_bias,
    merge_weight,
    merge_bias,
    up_weight,
    up_bias,
    down_weight,
    down_bias,
    modulate_weight,
    modulate_bias,
    relative_table,
    cotangent,
):
    position = lax.axis_index("seq")
    position_bias = jnp.take(relative_table, relative_index(jnp.arange(GRID)), axis=1)
    own_cond = lax.dynamic_slice_in_dim(condition, position * SAMP_DEV, SAMP_DEV, 0)
    own_silu = jax.nn.silu(own_cond.astype(jnp.float32)).astype(jnp.bfloat16)
    modulation = fold_rows(own_silu, lax.all_gather(modulate_weight, "seq", axis=0, tiled=True))
    modulation = (modulation + modulate_bias.astype(jnp.float32)).reshape(SAMP_DEV, 1, 6, D)
    full_bias = jnp.concatenate(
        [heads_bias[:D], jnp.zeros((D,), jnp.bfloat16), heads_bias[D:]]
    ).astype(jnp.float32)
    parts_count = MICRO
    samples = SAMP_DEV // parts_count
    rows = samples * GRID
    pairs = samples // 2
    kept = {
        "out": [],
        "tgrad": [],
        "mgrad": [],
        "hone": [],
        "gpack": [],
        "attn": [],
        "gbranch": [],
        "htwo": [],
        "gup": [],
        "gmlp": [],
        "act": [],
    }
    placed_total = jnp.zeros((HEADS, GRID, GRID), jnp.float32)
    for part in range(parts_count):
        slab = tokens[part * rows : (part + 1) * rows].astype(jnp.float32).reshape(samples, GRID, D)
        mods = modulation[part * samples : (part + 1) * samples]
        shift_one, scale_one, gate_one, shift_two, scale_two, gate_two = [
            mods[:, :, index] for index in range(6)
        ]
        lens_part = lengths[part * samples : (part + 1) * samples]
        index_part = kept_index[part * samples : (part + 1) * samples]
        living = (jnp.arange(GRID)[None, :] < lens_part[:, None])[:, :, None]
        hidden_one = modulated(slab, scale_one, shift_one).astype(jnp.bfloat16).reshape(rows, D)
        packed = (
            fold_rows(hidden_one, lax.all_gather(heads_weight, "seq", axis=0, tiled=True))
            + full_bias
        ).astype(jnp.bfloat16)
        packed_pairs = packed.reshape(pairs, 2 * GRID, 3 * D)
        lens_pairs = lens_part.reshape(pairs, 2)
        index_pairs = index_part.reshape(pairs, 2, GRID)
        attended, logsum = lax.map(
            partial(attend_pair, position_bias=position_bias),
            (packed_pairs, lens_pairs, index_pairs),
        )
        attended = attended.reshape(rows, D)
        branch = fold_rows(
            attended, lax.all_gather(merge_weight, "seq", axis=0, tiled=True)
        ) + merge_bias.astype(jnp.float32)
        branch = branch.reshape(samples, GRID, D)
        middle = slab + gate_one * branch
        hidden_two = modulated(middle, scale_two, shift_two).astype(jnp.bfloat16).reshape(rows, D)
        up_value = fold_rows(
            hidden_two, lax.all_gather(up_weight, "seq", axis=0, tiled=True)
        ) + up_bias.astype(jnp.float32)
        activated = gelu_tanh(up_value).astype(jnp.bfloat16)
        mlp_out = right_transposed(
            activated, lax.all_gather(down_weight, "seq", axis=0, tiled=True)
        )
        mlp_out = (mlp_out + down_bias.astype(jnp.float32)).reshape(samples, GRID, D)
        final = jnp.where(living, middle + gate_two * mlp_out, 0.0)
        kept["out"].append(final.astype(jnp.bfloat16).reshape(rows, D))
        grad_final = jnp.where(
            living,
            cotangent[part * rows : (part + 1) * rows]
            .astype(jnp.float32)
            .reshape(samples, GRID, D),
            0.0,
        )
        gate_two_grad = jnp.sum(grad_final * mlp_out, axis=1, keepdims=True)
        grad_mlp = (gate_two * grad_final).astype(jnp.bfloat16).reshape(rows, D)
        grad_act = fold_rows(grad_mlp, lax.all_gather(down_weight, "seq", axis=0, tiled=True))
        grad_up = jax.vjp(gelu_tanh, up_value)[1](grad_act)[0].astype(jnp.bfloat16)
        grad_hidden_two = right_transposed(
            grad_up, lax.all_gather(up_weight, "seq", axis=0, tiled=True)
        )
        middle_ln, scale_two_grad, shift_two_grad = jax.vjp(
            modulated, middle, scale_two, shift_two
        )[1](grad_hidden_two.reshape(samples, GRID, D))
        grad_middle = grad_final + middle_ln
        gate_one_grad = jnp.sum(grad_middle * branch, axis=1, keepdims=True)
        grad_branch = (gate_one * grad_middle).astype(jnp.bfloat16).reshape(rows, D)
        grad_attended = right_transposed(
            grad_branch, lax.all_gather(merge_weight, "seq", axis=0, tiled=True)
        ).astype(jnp.bfloat16)
        grad_packed, placed_parts = lax.map(
            partial(attend_pair_back, position_bias=position_bias),
            (
                packed_pairs,
                lens_pairs,
                index_pairs,
                logsum,
                grad_attended.reshape(pairs, 2 * GRID, D),
            ),
        )
        grad_packed = grad_packed.reshape(rows, 3 * D)
        placed_total = placed_total + jnp.sum(placed_parts, axis=0)
        grad_hidden_one = right_transposed(
            grad_packed, lax.all_gather(heads_weight, "seq", axis=0, tiled=True)
        )
        slab_ln, scale_one_grad, shift_one_grad = jax.vjp(modulated, slab, scale_one, shift_one)[1](
            grad_hidden_one.reshape(samples, GRID, D)
        )
        kept["tgrad"].append((grad_middle + slab_ln).reshape(rows, D))
        kept["mgrad"].append(
            jnp.concatenate(
                [
                    shift_one_grad,
                    scale_one_grad,
                    gate_one_grad,
                    shift_two_grad,
                    scale_two_grad,
                    gate_two_grad,
                ],
                axis=-1,
            ).reshape(samples, 6 * D)
        )
        kept["hone"].append(hidden_one)
        kept["gpack"].append(grad_packed)
        kept["attn"].append(attended)
        kept["gbranch"].append(grad_branch)
        kept["htwo"].append(hidden_two)
        kept["gup"].append(grad_up)
        kept["gmlp"].append(grad_mlp)
        kept["act"].append(activated)
    table_grad = offsets_table(placed_total)
    joined = {name: jnp.concatenate(items, axis=0) for name, items in kept.items()}
    mod_grad = joined["mgrad"].astype(jnp.bfloat16)
    pieces = [
        column_outer(joined["hone"], joined["gpack"]),
        column_outer(joined["attn"], joined["gbranch"]),
        column_outer(joined["htwo"], joined["gup"]),
        column_outer(joined["gmlp"], joined["act"]),
        column_outer(own_silu, mod_grad),
    ]
    summed = lax.psum_scatter(
        jnp.concatenate(pieces, axis=1).astype(jnp.bfloat16), "seq", scatter_dimension=0, tiled=True
    )
    share = lax.psum_scatter(summed, "dp", scatter_dimension=0, tiled=True).astype(jnp.float32)
    replicated = lax.all_gather(share.astype(jnp.bfloat16), "dp", axis=0, tiled=True).astype(
        share.dtype
    )
    packed_sums = jnp.sum(joined["gpack"], axis=0, dtype=jnp.float32)
    heads_part = jnp.concatenate([packed_sums[:D], packed_sums[2 * D :]])
    merge_part = jnp.sum(joined["gbranch"], axis=0, dtype=jnp.float32)
    up_part = jnp.sum(joined["gup"], axis=0, dtype=jnp.float32)
    down_part = jnp.sum(joined["gmlp"], axis=0, dtype=jnp.float32)
    modulate_part = jnp.sum(mod_grad, axis=0, dtype=jnp.float32)
    heads_total, merge_total, up_total, down_total, modulate_total, table_total = lax.psum(
        (heads_part, merge_part, up_part, down_part, modulate_part, table_grad), ("dp", "seq")
    )
    edges = [0, 3 * D, 4 * D, 4 * D + FF, 4 * D + 2 * FF, 10 * D + 2 * FF]
    return (
        joined["out"],
        joined["tgrad"],
        replicated[:, edges[0] : edges[1]],
        replicated[:, edges[1] : edges[2]],
        replicated[:, edges[2] : edges[3]],
        replicated[:, edges[3] : edges[4]],
        replicated[:, edges[4] : edges[5]],
        heads_total,
        merge_total,
        up_total,
        down_total,
        modulate_total,
        table_total,
    )


def solution(mesh):
    in_specs = (
        P(("dp", "seq"), None),
        P("dp", None),
        P(("dp", "seq")),
        P(("dp", "seq"), None),
        P("seq", None),
        P(),
        P("seq", None),
        P(),
        P("seq", None),
        P(),
        P("seq", None),
        P(),
        P("seq", None),
        P(),
        P(),
        P(("dp", "seq"), None),
    )
    out_specs = (
        P(("dp", "seq"), None),
        P(("dp", "seq"), None),
        P("seq", None),
        P("seq", None),
        P("seq", None),
        P("seq", None),
        P("seq", None),
        P(),
        P(),
        P(),
        P(),
        P(),
        P(),
    )
    return jax.shard_map(local, mesh=mesh, in_specs=in_specs, out_specs=out_specs, check_vma=False)
```

profile of v0, /device:TPU:8, one launch (start us, length us, event | category | flops | bytes accessed | tf_op | source)
XLA Modules:
  0.0 2067.6 jit_solution(3447131822799105786)
XLA Ops:
  21.8 4.3 slice_convert_fusion.1
  26.2 227.7 %gather_fusion = bf16[65536,16]{1,0:T(8,128)(2,1)} fusion(bf16[16,961]{0,1:T(8,128)(2,1)S(1)} %copy.147, s32[65536]{0:T(1024)S(1)} %broadcast_clamp_fusion), kind=kCustom, calls=%fused_computation | custom fusion | bytes 4456448 | tf_op jit(solution)/shard_map/jit(_take)/gather | solution.py:168
  253.8 16.7 copy.148
  270.6 5.1 convert_bitcast_fusion
  279.7 7.9 convolution_add_fusion
  292.3 54.5 %all-gather.10.cloned.1.call-done = bf16[1152,3456]{1,0:T(8,128)(2,1)} async-done(((bf16[144,3456]{1,0:T(8,128)(2,1)}), bf16[1152,3456]{1,0:T(8,128)(2,1)}) %all-gather.10.cloned.1.call-update) | async-done | bytes 7962640 | tf_op jit(solution)/shard_map/all_gather | solution.py:205
  346.7 9.5 add_convert_fusion.1
  356.3 5.8 copy.143
  362.1 8.3 reshape.859
  370.4 15.9 fusion.217
  399.5 4.5 all-gather.12.cloned.1.call-done
  404.0 6.8 fusion.212
  411.4 11.2 add_convert_fusion
  422.6 5.7 copy.152
  428.3 8.3 reshape.861
  467.8 87.5 %all-gather.14.cloned.1.call-done = bf16[1152,4608]{1,0:T(8,128)(2,1)} async-done(((bf16[144,4608]{1,0:T(8,128)(2,1)}), bf16[1152,4608]{1,0:T(8,128)(2,1)}) %all-gather.14.cloned.1.call-update) | async-done | bytes 10616848 | tf_op jit(solution)/shard_map/all_gather | solution.py:223
  555.3 11.7 fusion.231
  566.9 8.9 fusion.230
  575.8 132.2 %all-gather.16.cloned.1.call-done = bf16[1152,4608]{1,0:T(8,128)(2,1)} async-done(((bf16[144,4608]{1,0:T(8,128)(2,1)}), bf16[1152,4608]{1,0:T(8,128)(2,1)}) %all-gather.16.cloned.1.call-update) | async-done | bytes 10616848 | tf_op jit(solution)/shard_map/all_gather | solution.py:227
  708.0 11.6 fusion.232
  719.6 24.2 %fusion.11 = (bf16[512,4608]{1,0:T(8,128)(2,1)}, bf16[512,4608]{1,0:T(8,128)(2,1)}, bf16[512,4608]{1,0:T(8,128)(2,1)}, bf16[512,4608]{1,0:T(8,128)(2,1)}) fusion(f32[512,4608]{1,0:T(8,128)} %fusion.230, f32[4608]{0:T(1024)S(1)} %copy-done.104, f32[512,4608]{1,0:T(8,128)} %fusion.231, f32[512,4608]{1,0:T(8,128)} %fusion.232, ...), kind=kOutput, calls=%fused_computation.21 | convolution fusion | flops 5544345600 | bytes 59000832 | tf_op jit(solution)/shard_map/dot_general | solution.py:34
  743.8 12.7 multiply_reduce_fusion.11
  757.2 13.2 multiply_reduce_fusion.9
  771.0 14.4 fusion.210
  785.5 13.1 fusion.211
  810.9 5.3 multiply_reduce_fusion.1
  832.8 4.8 convolution_convert_fusion.4
  847.4 6.1 multiply_reduce_fusion
  864.9 5.5 copy.182
  874.3 5.2 copy.183
  883.6 8.8 multiply_reduce_fusion.10
  899.8 10.3 multiply_reduce_fusion.8
  910.2 4.8 multiply_reduce_fusion.4
  916.6 10.9 fusion.4
  931.0 17.3 fusion.3
  948.4 16.6 fusion.2
  975.5 8.7 fusion.1
  984.2 748.7 %reduce-scatter.4.cloned.1.call-done = bf16[144,20736]{1,0:T(8,128)(2,1)} async-done(((bf16[1152,20736]{1,0:T(8,128)(2,1)}), bf16[144,20736]{1,0:T(8,128)(2,1)}) %reduce-scatter.4.cloned.1.call-update) | async-done | bytes 5971984 | tf_op jit(solution)/shard_map/reduce_scatter | solution.py:305
  1732.9 62.0 %fusion = bf16[40,20736]{1,0:T(8,128)(2,1)} fusion(bf16[144,20736]{1,0:T(8,128)(2,1)} %reduce-scatter.4.cloned.1.call-done), kind=kCustom, calls=%all-reduce-scatter | all-reduce-scatter fusion | flops 3317761 | bytes 7631360
  1800.4 17.0 concatenate.72
  1820.6 6.8 fusion.32
  1827.4 8.1 bitcast_add_fusion.2
  1835.4 19.8 add.547
  1855.2 33.3 %fusion.185 = f32[31,16,16,16,1]{0,3,2,4,1:T(8,128)} fusion(f32[16,16,16,16,16]{4,3,2,1,0:T(8,128)} %add.547, s32[16,16]{1,0:T(8,128)S(1)} %subtract_add_fusion), kind=kOutput, calls=%fused_computation.258 | convolution fusion | flops 390078208 | bytes 4703232 | tf_op jit(solution)/shard_map/hwxyz,wya->haxz/dot_general | solution.py:143
  1911.9 4.3 convert_reduce_fusion
  1916.3 10.3 reshape.899
  1926.6 5.7 fusion.216
  1938.7 113.8 %all-reduce.5.cloned.1.call-done = (f32[2304]{0:T(1024)}, f32[1152]{0:T(1024)}, f32[4608]{0:T(1024)}, f32[1152]{0:T(1024)}, f32[6912]{0:T(1024)}, /*index=5*/f32[16,961]{1,0:T(8,128)}) async-done(((f32[2304]{0:T(1024)}, f32[1152]{0:T(1024)}, f32[4608]{0:T(1024)}, f32[1152]{0:T(1024)}, f32[6912]{0:T(1024)}, /*index=5*/f32[16,961]{1,0:T(8,128)}), (f32[2304]{0:T(1024)}, f32[1152]{0:T(1024)}, f32[4608]{0:T(1024)}, ...) | async-done | bytes 126032 | tf_op jit(solution)/shard_map/psum | solution.py:318
  (496 shorter events, 194.9 us)
Async XLA Ops:
  7.2 272.5 %all-gather.8.cloned.1.call-start = ((), (), s32[]{:S(2)}) async-start(), calls=%async_computation.1 | async-start | bytes 17915904 | tf_op jit(solution)/shard_map/all_gather | solution.py:171
  7.9 338.8 %all-gather.10.cloned.1.call-start = ((), (), s32[]{:S(2)}) async-start(), calls=%async_computation.2 | async-start | bytes 8957952 | tf_op jit(solution)/shard_map/all_gather | solution.py:205
  8.7 395.3 %all-gather.12.cloned.1.call-start = ((), (), s32[]{:S(2)}) async-start(), calls=%async_computation.3 | async-start | bytes 2985984 | tf_op jit(solution)/shard_map/all_gather | solution.py:217
  9.4 545.9 %all-gather.14.cloned.1.call-start = ((), (), s32[]{:S(2)}) async-start(), calls=%async_computation.4 | async-start | bytes 11943936 | tf_op jit(solution)/shard_map/all_gather | solution.py:223
  10.0 698.0 %all-gather.16.cloned.1.call-start = ((), (), s32[]{:S(2)}) async-start(), calls=%async_computation.5 | async-start | bytes 11943936 | tf_op jit(solution)/shard_map/all_gather | solution.py:227
  10.6 1722.4 %reduce-scatter.4.cloned.1.call-start = ((), (), s32[]{:S(2)}) async-start(), calls=%async_computation.6 | async-start | bytes 53747712 | tf_op jit(solution)/shard_map/reduce_scatter | solution.py:305
  17.2 253.4 %copy-start.135 = (s32[2,256]{1,0:T(2,128)}, s32[2,256]{1,0:T(2,128)S(1)}, u32[]{:S(2)}) copy-start(s32[2,256]{1,0:T(2,128)S(1)} %get-tuple-element.193) | copy-start | bytes 6148
  17.2 370.5 %copy-start.98 = (s32[2,256]{1,0:T(2,128)}, s32[2,256]{1,0:T(2,128)S(1)}, u32[]{:S(2)}) copy-start(s32[2,256]{1,0:T(2,128)S(1)} %get-tuple-element.192) | copy-start | bytes 6148
  292.3 64.0 %copy-start.63 = (bf16[512,1152]{1,0:T(8,128)(2,1)}, bf16[512,1152]{1,0:T(8,128)(2,1)S(1)}, u32[]{:S(2)}) copy-start(bf16[512,1152]{1,0:T(8,128)(2,1)S(1)} %fusion.98) | copy-start | bytes 3538948
  398.8 12.0 copy-start.54
  399.5 11.3 copy-start.70
  461.2 309.8 %copy-start.74 = (f32[2,1152]{1,0:T(2,128)}, f32[2,1152]{1,0:T(2,128)S(1)}, u32[]{:S(2)}) copy-start(f32[2,1152]{1,0:T(2,128)S(1)} %get-tuple-element.239) | copy-start | bytes 27652
  464.0 321.5 %copy-start.81 = (f32[2,1152]{1,0:T(2,128)}, f32[2,1152]{1,0:T(2,128)S(1)}, u32[]{:S(2)}) copy-start(f32[2,1152]{1,0:T(2,128)S(1)} %get-tuple-element.235) | copy-start | bytes 27652
  555.3 11.7 copy-start.66
  555.3 11.7 copy-start.155
  708.0 11.6 copy-start.5
  708.0 11.6 copy-start.104
  757.2 13.2 copy-start.110
  757.2 13.8 copy-start.88
  757.2 13.8 copy-start.108
  757.2 13.8 copy-start.149
  771.0 14.5 copy-start.10
  771.0 14.5 copy-start.11
  771.0 14.5 copy-start.106
  771.0 14.5 copy-start.147
  785.5 14.2 copy-start.71
  883.5 8.9 copy-start.139
  883.5 8.9 copy-start.1
  883.5 8.9 copy-start.13
  883.5 8.9 copy-start.15
  883.6 8.9 copy-start.114
  899.8 10.3 copy-start.138
  899.8 10.4 copy-start.12
  899.8 10.4 copy-start.14
  899.8 10.4 copy-start.73
  899.8 10.4 copy-start.115
  916.6 10.9 copy-start.17
  931.0 17.3 copy-start.52
  948.3 16.7 copy-start.75
  948.3 16.7 copy-start.126
  948.3 16.7 copy-start.134
  984.2 815.0 %copy-start.154 = (u32[32]{0:T(128)S(1)}, u32[32]{0:T(128)}, u32[]{:S(2)}) copy-start(u32[32]{0:T(128)} %constant.195) | copy-start | bytes 388
  984.2 932.1 %all-gather.18.cloned.1.call-start = ((), (), s32[]{:S(2)}) async-start(), calls=%async_computation.7 | async-start | bytes 8294400 | tf_op jit(solution)/shard_map/all_gather | solution.py:309
  1797.0 3.4 collective-permute-start
  1820.5 232.0 %all-reduce.5.cloned.1.call-start = ((), (), s32[]{:S(2)}) async-start(), calls=%async_computation.8 | async-start | bytes 286720 | tf_op jit(solution)/shard_map/psum | solution.py:318
  1896.0 8.5 copy-start.77
  1896.0 8.5 copy-start.80
  1926.6 8.5 copy-start.4
  (123 other events, 456.9 us)
Sparse Core Ops, SparseCore 0:
  10.2 216.5 all-gather.7
  228.9 117.7 all-gather.9
  348.9 55.0 all-gather.11
  406.0 149.1 all-gather.13
  557.3 150.6 all-gather.15
  984.3 748.6 reduce-scatter.3
  1820.6 57.1 all-gather.17
  1916.3 136.0 all-reduce.4
where the time goes:
time: 2070 us
  waiting for transfers between devices  1140 us (55%)
  local copies, waits for them, and re-layouts  442 us (21%)
  matrix products  327 us (16%)
  other arithmetic  72.9 us (4%)
  blocking collectives  62 us (3%)
    reduce_scatter x1, waiting for transfers between devices, local(): lax.psum_scatter(jnp.concatenate(pieces, axis=1).astype(jnp.bfloat16), 's...  749 us
    gather x2, local copies, waits for them, and re-layouts, local(): jnp.take(relative_table, relative_index(jnp.arange(GRID)), axis=1)  244 us
    all_gather x1, waiting for transfers between devices, local(): lax.all_gather(down_weight, 'seq', axis=0, tiled=True)  132 us
    psum x1, waiting for transfers between devices, local(): lax.psum((heads_part, merge_part, up_part, down_part, modulate_part, tabl...  114 us
    dot_general x9, matrix products, fold_rows(): return jnp.dot(left, portion, preferred_element_type=jnp.float32)  96.1 us
    all_gather x1, waiting for transfers between devices, local(): lax.all_gather(up_weight, 'seq', axis=0, tiled=True)  87.5 us
    dot_general x8, matrix products, right_transposed(): lax.dot_general(left, portion, (((1,), (1,)), ((), ())), preferred_elemen...  77.3 us
    unnamed x359, local copies, waits for them, and re-layouts  65.2 us
  transfers between devices with their start and end apart: 9, of which 6 were waited for; matrix products, arithmetic and copies ran while one was open for 25% of the time, Pallas kernels for 0%

commit v1 on v0

--- a/solution.py
+++ b/solution.py
@@ -316,7 +316,8 @@
     down_part = jnp.sum(joined["gmlp"], axis=0, dtype=jnp.float32)
     modulate_part = jnp.sum(mod_grad, axis=0, dtype=jnp.float32)
     heads_total, merge_total, up_total, down_total, modulate_total, table_total = lax.psum(
-        (heads_part, merge_part, up_part, down_part, modulate_part, table_grad), ("dp", "seq")
+        lax.psum((heads_part, merge_part, up_part, down_part, modulate_part, table_grad), "seq"),
+        "dp",
     )
     edges = [0, 3 * D, 4 * D, 4 * D + FF, 4 * D + 2 * FF, 10 * D + 2 * FF]
     return (

time: 2070 us -> 1980 us (0.957)
  waiting for transfers between devices: 1140 us -> 1050 us
    reduce_scatter x1, waiting for transfers between devices: 749 us -> 668 us  [local(): lax.psum_scatter(jnp.concatenate(pieces, axis=1).astype(jnp.bfloat16), 's...]
    psum x1, waiting for transfers between devices: 114 us -> 43.3 us  [local(): lax.psum((heads_part, merge_part, up_part, down_part, modulate_part, tabl...]
    all_gather x1, waiting for transfers between devices: 0.02 us -> 50.5 us  [local(): lax.all_gather(share.astype(jnp.bfloat16), 'dp', axis=0, tiled=True)]
    unnamed x359 -> x337, local copies, waits for them, and re-layouts: 65.2 us -> 61.1 us
  transfers between devices with their start and end apart: 9 -> 10, of which waited for: 6 -> 8; matrix products, arithmetic and copies ran while one was open for 25% -> 28% of each run, Pallas kernels for 0% -> 0%
where the time goes in v1:
time: 1980 us
  waiting for transfers between devices  1050 us (53%)
  local copies, waits for them, and re-layouts  439 us (22%)
  matrix products  326 us (16%)
  other arithmetic  79.3 us (4%)
  blocking collectives  61.9 us (3%)
    reduce_scatter x1, waiting for transfers between devices, local(): lax.psum_scatter(jnp.concatenate(pieces, axis=1).astype(jnp.bfloat16), 's...  668 us
    gather x2, local copies, waits for them, and re-layouts, local(): jnp.take(relative_table, relative_index(jnp.arange(GRID)), axis=1)  246 us
    all_gather x1, waiting for transfers between devices, local(): lax.all_gather(down_weight, 'seq', axis=0, tiled=True)  132 us
    dot_general x9, matrix products, fold_rows(): return jnp.dot(left, portion, preferred_element_type=jnp.float32)  95.9 us
    all_gather x1, waiting for transfers between devices, local(): lax.all_gather(up_weight, 'seq', axis=0, tiled=True)  87.5 us
    dot_general x8, matrix products, right_transposed(): lax.dot_general(left, portion, (((1,), (1,)), ((), ())), preferred_elemen...  77.2 us
    unnamed x1, blocking collectives  61.9 us
    unnamed x337, local copies, waits for them, and re-layouts  61.1 us
  transfers between devices with their start and end apart: 10, of which 8 were waited for; matrix products, arithmetic and copies ran while one was open for 28% of the time, Pallas kernels for 0%

profile of v1, /device:TPU:8, one launch (start us, length us, event | category | flops | bytes accessed | tf_op | source)
XLA Modules:
  0.0 1976.9 jit_solution(18083044827375722875)
XLA Ops:
  26.3 229.3 %gather_fusion = bf16[65536,16]{1,0:T(8,128)(2,1)} fusion(bf16[16,961]{0,1:T(8,128)(2,1)S(1)} %copy.147, s32[65536]{0:T(1024)S(1)} %broadcast_clamp_fusion), kind=kCustom, calls=%fused_computation | custom fusion | bytes 4456448 | tf_op jit(solution)/shard_map/jit(_take)/gather | solution.py:168
  255.7 16.7 copy.148
  272.4 5.1 convert_bitcast_fusion
  281.5 7.8 convolution_add_fusion
  294.0 52.8 %all-gather.10.cloned.1.call-done = bf16[1152,3456]{1,0:T(8,128)(2,1)} async-done(((bf16[144,3456]{1,0:T(8,128)(2,1)}), bf16[1152,3456]{1,0:T(8,128)(2,1)}) %all-gather.10.cloned.1.call-update) | async-done | bytes 7962640 | tf_op jit(solution)/shard_map/all_gather | solution.py:205
  346.7 9.5 add_convert_fusion.1
  356.3 5.8 copy.143
  362.1 8.3 reshape.859
  370.4 15.9 fusion.217
  404.0 6.8 fusion.212
  411.4 11.2 add_convert_fusion
  422.6 5.7 copy.152
  428.4 8.3 reshape.861
  467.8 87.5 %all-gather.14.cloned.1.call-done = bf16[1152,4608]{1,0:T(8,128)(2,1)} async-done(((bf16[144,4608]{1,0:T(8,128)(2,1)}), bf16[1152,4608]{1,0:T(8,128)(2,1)}) %all-gather.14.cloned.1.call-update) | async-done | bytes 10616848 | tf_op jit(solution)/shard_map/all_gather | solution.py:223
  555.3 11.7 fusion.231
  566.9 8.9 fusion.230
  575.8 132.2 %all-gather.16.cloned.1.call-done = bf16[1152,4608]{1,0:T(8,128)(2,1)} async-done(((bf16[144,4608]{1,0:T(8,128)(2,1)}), bf16[1152,4608]{1,0:T(8,128)(2,1)}) %all-gather.16.cloned.1.call-update) | async-done | bytes 10616848 | tf_op jit(solution)/shard_map/all_gather | solution.py:227
  708.0 11.6 fusion.232
  719.6 24.2 %fusion.11 = (bf16[512,4608]{1,0:T(8,128)(2,1)}, bf16[512,4608]{1,0:T(8,128)(2,1)}, bf16[512,4608]{1,0:T(8,128)(2,1)}, bf16[512,4608]{1,0:T(8,128)(2,1)}) fusion(f32[512,4608]{1,0:T(8,128)} %fusion.230, f32[4608]{0:T(1024)S(1)} %copy-done.101, f32[512,4608]{1,0:T(8,128)} %fusion.231, f32[512,4608]{1,0:T(8,128)} %fusion.232, ...), kind=kOutput, calls=%fused_computation.21 | convolution fusion | flops 5544345600 | bytes 59000832 | tf_op jit(solution)/shard_map/dot_general | solution.py:34
  743.8 12.7 multiply_reduce_fusion.11
  757.1 13.1 multiply_reduce_fusion.9
  770.9 14.4 fusion.210
  785.4 13.1 fusion.211
  810.8 5.1 multiply_reduce_fusion.1
  832.7 4.8 convolution_convert_fusion.4
  847.3 6.1 multiply_reduce_fusion
  864.7 5.4 copy.182
  874.0 5.2 copy.183
  883.3 8.8 multiply_reduce_fusion.10
  899.6 10.3 multiply_reduce_fusion.8
  910.0 4.7 multiply_reduce_fusion.4
  916.4 10.9 fusion.4
  930.8 17.2 fusion.3
  948.1 16.7 fusion.2
  975.2 8.6 fusion.1
  985.8 7.2 fusion.32
  993.0 8.0 bitcast_add_fusion.2
  1001.0 19.6 add.559
  1024.0 33.4 %fusion.185 = f32[31,16,16,16,1]{0,3,2,4,1:T(8,128)} fusion(f32[16,16,16,16,16]{4,3,2,1,0:T(8,128)} %add.559, s32[16,16]{1,0:T(8,128)S(1)} %subtract_add_fusion), kind=kOutput, calls=%fused_computation.258 | convolution fusion | flops 390078208 | bytes 4703232 | tf_op jit(solution)/shard_map/hwxyz,wya->haxz/dot_general | solution.py:143
  1065.0 667.7 %reduce-scatter.4.cloned.1.call-done = bf16[144,20736]{1,0:T(8,128)(2,1)} async-done(((bf16[1152,20736]{1,0:T(8,128)(2,1)}), bf16[144,20736]{1,0:T(8,128)(2,1)}) %reduce-scatter.4.cloned.1.call-update) | async-done | bytes 5971984 | tf_op jit(solution)/shard_map/reduce_scatter | solution.py:305
  1732.6 61.9 %fusion = bf16[40,20736]{1,0:T(8,128)(2,1)} fusion(bf16[144,20736]{1,0:T(8,128)(2,1)} %reduce-scatter.4.cloned.1.call-done), kind=kCustom, calls=%all-reduce-scatter | all-reduce-scatter fusion | flops 3317761 | bytes 7631360
  1800.1 5.7 convert_reduce_fusion
  1805.9 14.9 concatenate.72
  1834.5 43.3 %all-reduce.7.cloned.1.call-done = (f32[2304]{0:T(1024)}, f32[1152]{0:T(1024)}, f32[4608]{0:T(1024)}, f32[1152]{0:T(1024)}, f32[6912]{0:T(1024)}, /*index=5*/f32[16,961]{1,0:T(8,128)}) async-done(((f32[2304]{0:T(1024)}, f32[1152]{0:T(1024)}, f32[4608]{0:T(1024)}, f32[1152]{0:T(1024)}, f32[6912]{0:T(1024)}, /*index=5*/f32[16,961]{1,0:T(8,128)}), (f32[2304]{0:T(1024)}, f32[1152]{0:T(1024)}, f32[4608]{0:T(1024)}, ...) | async-done | bytes 126032 | tf_op jit(solution)/shard_map/psum | solution.py:319
  1877.8 50.5 %all-gather.18.cloned.1.call-done = bf16[4,36,20736]{2,1,0:T(8,128)(2,1)} async-done(((bf16[1,36,20736]{2,1,0:T(8,128)(2,1)}), bf16[4,36,20736]{2,1,0:T(8,128)(2,1)}) %all-gather.18.cloned.1.call-update) | async-done | bytes 5971984 | tf_op jit(solution)/shard_map/all_gather | solution.py:309
  1928.3 10.4 reshape.899
  1938.7 5.8 fusion.216
  1950.8 11.3 all-reduce.9.cloned.1.call-done
  (476 shorter events, 204.3 us)
Async XLA Ops:
  7.2 274.3 %all-gather.8.cloned.1.call-start = ((), (), s32[]{:S(2)}) async-start(), calls=%async_computation.1 | async-start | bytes 17915904 | tf_op jit(solution)/shard_map/all_gather | solution.py:171
  7.9 338.8 %all-gather.10.cloned.1.call-start = ((), (), s32[]{:S(2)}) async-start(), calls=%async_computation.2 | async-start | bytes 8957952 | tf_op jit(solution)/shard_map/all_gather | solution.py:205
  8.7 395.3 %all-gather.12.cloned.1.call-start = ((), (), s32[]{:S(2)}) async-start(), calls=%async_computation.3 | async-start | bytes 2985984 | tf_op jit(solution)/shard_map/all_gather | solution.py:217
  9.4 545.9 %all-gather.14.cloned.1.call-start = ((), (), s32[]{:S(2)}) async-start(), calls=%async_computation.4 | async-start | bytes 11943936 | tf_op jit(solution)/shard_map/all_gather | solution.py:223
  10.0 698.0 %all-gather.16.cloned.1.call-start = ((), (), s32[]{:S(2)}) async-start(), calls=%async_computation.5 | async-start | bytes 11943936 | tf_op jit(solution)/shard_map/all_gather | solution.py:227
  10.6 1722.1 %reduce-scatter.4.cloned.1.call-start = ((), (), s32[]{:S(2)}) async-start(), calls=%async_computation.6 | async-start | bytes 53747712 | tf_op jit(solution)/shard_map/reduce_scatter | solution.py:305
  17.3 255.1 %copy-start.128 = (s32[2,256]{1,0:T(2,128)}, s32[2,256]{1,0:T(2,128)S(1)}, u32[]{:S(2)}) copy-start(s32[2,256]{1,0:T(2,128)S(1)} %get-tuple-element.199) | copy-start | bytes 6148
  17.3 370.4 %copy-start.95 = (s32[2,256]{1,0:T(2,128)}, s32[2,256]{1,0:T(2,128)S(1)}, u32[]{:S(2)}) copy-start(s32[2,256]{1,0:T(2,128)S(1)} %get-tuple-element.198) | copy-start | bytes 6148
  293.9 62.3 %copy-start.59 = (bf16[512,1152]{1,0:T(8,128)(2,1)}, bf16[512,1152]{1,0:T(8,128)(2,1)S(1)}, u32[]{:S(2)}) copy-start(bf16[512,1152]{1,0:T(8,128)(2,1)S(1)} %fusion.98) | copy-start | bytes 3538948
  398.8 12.0 copy-start.50
  399.5 11.3 copy-start.66
  461.2 309.6 %copy-start.70 = (f32[2,1152]{1,0:T(2,128)}, f32[2,1152]{1,0:T(2,128)S(1)}, u32[]{:S(2)}) copy-start(f32[2,1152]{1,0:T(2,128)S(1)} %get-tuple-element.245) | copy-start | bytes 27652
  464.0 321.3 %copy-start.76 = (f32[2,1152]{1,0:T(2,128)}, f32[2,1152]{1,0:T(2,128)S(1)}, u32[]{:S(2)}) copy-start(f32[2,1152]{1,0:T(2,128)S(1)} %get-tuple-element.241) | copy-start | bytes 27652
  555.3 11.7 copy-start.62
  555.3 11.7 copy-start.146
  708.0 11.6 copy-start.5
  708.0 11.6 copy-start.101
  757.1 13.1 copy-start.107
  757.1 13.8 copy-start.85
  757.1 13.8 copy-start.105
  757.1 13.8 copy-start.140
  770.9 14.4 copy-start.10
  770.9 14.4 copy-start.11
  770.9 14.4 copy-start.103
  770.9 14.4 copy-start.138
  785.4 14.3 copy-start.67
  883.3 8.9 copy-start.132
  883.3 8.9 copy-start.1
  883.3 8.9 copy-start.13
  883.3 8.9 copy-start.15
  883.3 8.9 copy-start.111
  899.5 10.3 copy-start.131
  899.5 10.4 copy-start.12
  899.5 10.4 copy-start.14
  899.5 10.4 copy-start.69
  899.6 10.4 copy-start.112
  916.4 10.9 copy-start.17
  930.8 17.2 copy-start.49
  948.0 16.7 copy-start.71
  948.0 16.7 copy-start.119
  948.0 16.7 copy-start.127
  983.9 893.9 %all-reduce.7.cloned.1.call-start = ((), (), s32[]{:S(2)}) async-start(), calls=%async_computation.8 | async-start | bytes 286720 | tf_op jit(solution)/shard_map/psum | solution.py:319
  1064.9 734.5 %copy-start.82 = (bf16[2,1,6912]{2,0,1:T(2,128)(2,1)S(1)}, bf16[2,1,6912]{2,0,1:T(2,128)(2,1)}, u32[]{:S(2)}) copy-start(bf16[2,1,6912]{2,0,1:T(2,128)(2,1)} %copy-done.81) | copy-start | bytes 82948
  1064.9 734.4 %copy-start.84 = (bf16[2,1,6912]{2,0,1:T(2,128)(2,1)S(1)}, bf16[2,1,6912]{2,0,1:T(2,128)(2,1)}, u32[]{:S(2)}) copy-start(bf16[2,1,6912]{2,0,1:T(2,128)(2,1)} %copy-done.83) | copy-start | bytes 82948
  1796.7 9.3 collective-permute-start
  1805.9 122.5 %all-gather.18.cloned.1.call-start = ((), (), s32[]{:S(2)}) async-start(), calls=%async_computation.7 | async-start | bytes 8294400 | tf_op jit(solution)/shard_map/all_gather | solution.py:309
  1824.1 138.0 %all-reduce.9.cloned.1.call-start = ((), (), s32[]{:S(2)}) async-start(), calls=%async_computation.9 | async-start | bytes 286720 | tf_op jit(solution)/shard_map/psum | solution.py:318
  1938.7 8.5 copy-start.4
  (113 other events, 411.4 us)
Sparse Core Ops, SparseCore 0:
  10.2 216.5 all-gather.7
  228.9 117.7 all-gather.9
  348.9 55.0 all-gather.11
  406.0 149.1 all-gather.13
  557.3 150.6 all-gather.15
  984.0 748.5 reduce-scatter.3
  1806.0 71.7 all-reduce.6
  1880.0 48.2 all-gather.17
  1931.3 30.7 all-reduce.8
